TPU v7x, 512 devices: a whole 4x4x16 slice. The times are simulated.
512 devices in a mesh: head: 16 (over y, x), tok: 32 (over z, core).
Axes of the slice: x: 4, y: 4, z: 16, core: 2. Of those that a mesh axis runs over, the one named last changes fastest.
Arguments:
- stretch_tokens: bfloat16 [32, 1024, 1792], P('tok', 'head'), may hold values from -6 to 6
- stretch_tail: bfloat16 [32, 2, 1792], P('tok'), may hold values from -6 to 6
- decode_tokens: bfloat16 [32, 32, 1792], P('tok'), may hold values from -6 to 6
- decode_tail: bfloat16 [32, 32, 2, 1792], P('tok'), may hold values from -6 to 6
- norm_gain: float32 [1792], replicated, may hold values from 0.1 to 1.9
- conv_taps: float32 [3, 1792], replicated, may hold values from -3 to 3
- qkv_weight: bfloat16 [1792, 16, 144], P(None, 'head'), may hold values from -0.125 to 0.125
- out_gain: float32 [1792], P('head'), may hold values from 0.1 to 1.9
- out_weight: bfloat16 [1792, 1792], P('head'), may hold values from -0.125 to 0.125
- state_cache: float32 [32, 16, 16, 112, 273], P('tok', None, 'head'), may hold values from -24 to 24
- stretch_len: int32 [32], P('tok'), may hold values from 1 to 1024, 16384 in all
- stretch_slot: int32 [32], P('tok'), may hold values from 0 to 15
- decode_slot: int32 [32, 32], P('tok'), may hold values from 0 to 15
- decode_owner: int32 [32, 32, 1], P('tok'), may hold values from 0 to 31; in each aligned block of 32 rows (0 to 31, 32 to 63, ..., all dimensions but the last counted through in order) at most 2 rows name the same one
Outputs:
- stretch_out: bfloat16 [32, 1024, 1792], P('tok', 'head')
- decode_out: bfloat16 [32, 32, 1792], P('tok', 'head')
- state_new: float32 [32, 16, 112, 273], P('tok', 'head')
Inputs may be any that keep to these rules, and one draw needn't show every extreme that they name: `decode_owner`: in the 32 decoders of one group at most 2 name the same owner group, a bound that some block reaches of them. `stretch_len`: some group's stretch is full.
All inputs are finite; a program needn't handle non-finite values.
Results may differ from a plain program's by a relative error of at most 0.014.
Values may be sent and summed in bfloat16 or wider, within the bound.
A program may use at most 64 MiB of HBM per device.

v0:
```python
import math
import jax
import jax.numpy as jnp
from jax import lax
from jax.sharding import PartitionSpec as P

D = 1792
DH = 112
F = 16
STRETCH = 1024
DEC = 32


def from_behind(array, axis, by):
    peers = lax.axis_size(axis)
    pairs = [(i, i + by) for i in range(peers) if 0 <= i + by < peers]
    return lax.ppermute(array, axis, pairs)


def rms_rows(values, gain):
    values = values.astype(jnp.float32)
    factor = lax.rsqrt(jnp.mean(values * values, axis=-1, keepdims=True) + 1e-05)
    return values * factor * gain


def features(vectors):
    breadth = vectors.shape[-1]
    linear = vectors / math.sqrt(math.sqrt(breadth))
    outer = vectors[..., :, None] * vectors[..., None, :] / math.sqrt(2.0 * breadth)
    outer = outer.reshape(vectors.shape[:-1] + (breadth * breadth,))
    ones = jnp.ones(vectors.shape[:-1] + (1,), vectors.dtype)
    return jnp.concatenate([ones, linear, outer], axis=-1)


def convolve(tail, normed, conv_taps):
    joined = jnp.concatenate([tail, normed], axis=-2).astype(jnp.float32)
    span_rows = normed.shape[-2]
    total = conv_taps[0] * joined[..., 0:span_rows, :]
    total = total + conv_taps[1] * joined[..., 1 : span_rows + 1, :]
    total = total + conv_taps[2] * joined[..., 2 : span_rows + 2, :]
    return total.astype(jnp.bfloat16)


def decode_items(items, slot_items, cache_own, out_gain, head_count):
    item_count = items.shape[0]
    shaped = items.reshape(item_count, head_count, 2 * F + DH).astype(jnp.float32)
    queries = shaped[:, :, :F]
    key_feats = shaped[:, :, F : 2 * F]
    values = shaped[:, :, 2 * F :]
    slot_total = cache_own.shape[0]
    table = jnp.einsum(
        "nhp,shdp->nshd", features(queries), cache_own, precision=lax.Precision.HIGHEST
    )
    picker = (slot_items[:, None] == jnp.arange(slot_total)[None, :]).astype(jnp.float32)
    carried = jnp.einsum("ns,nshd->nhd", picker, table, precision=lax.Precision.HIGHEST)
    inner = jnp.sum(queries * key_feats, axis=-1) / math.sqrt(F)
    own_term = (1.0 + inner + 0.5 * inner * inner)[..., None] * values
    attended = rms_rows(carried + own_term, out_gain.reshape(head_count, DH))
    return attended.astype(jnp.bfloat16).reshape(item_count, head_count * DH)


def local(
    stretch_tokens,
    stretch_tail,
    decode_tokens,
    decode_tail,
    norm_gain,
    conv_taps,
    qkv_weight,
    out_gain,
    out_weight,
    state_cache,
    stretch_len,
    stretch_slot,
    decode_slot,
    decode_owner,
):
    head_count = qkv_weight.shape[1]
    block_width = qkv_weight.shape[2]
    rows_own = stretch_tokens.shape[1]
    w_flat = qkv_weight.reshape(D, head_count * block_width)
    gains = out_gain.reshape(head_count, DH)
    normed = rms_rows(stretch_tokens[0], norm_gain).astype(jnp.bfloat16)
    rim_rows = from_behind(normed[rows_own - 2 :], "head", 1)
    first_dev = lax.axis_index("head") == 0
    rim_rows = jnp.where(first_dev, stretch_tail[0], rim_rows)
    conved = convolve(rim_rows, normed, conv_taps)
    grouped = jnp.dot(
        lax.all_gather(conved, "head", axis=0, tiled=True),
        w_flat,
        preferred_element_type=jnp.float32,
    ).astype(jnp.bfloat16)
    grouped = grouped.reshape(STRETCH, head_count, block_width)
    queries = grouped[:, :, :F]
    key_feats = grouped[:, :, F : 2 * F]
    values = grouped[:, :, 2 * F :]
    length = stretch_len[0]
    positions = jnp.arange(STRETCH)
    valid_rows = positions < length
    state_old = lax.dynamic_index_in_dim(state_cache[0], stretch_slot[0], 0, keepdims=False)
    carried = jnp.einsum(
        "ihp,hdp->ihd",
        features(queries.astype(jnp.float32)),
        state_old,
        precision=lax.Precision.HIGHEST,
    )
    block_rows = min(512, STRETCH)
    pieces = []
    for anchor in range(0, STRETCH, block_rows):
        finish = anchor + block_rows
        inner = jnp.einsum(
            "ihf,jhf->hij",
            queries[anchor:finish],
            key_feats[:finish],
            preferred_element_type=jnp.float32,
        ) / math.sqrt(F)
        weights = 1.0 + inner + 0.5 * inner * inner
        allowed = (positions[None, :finish] <= positions[anchor:finish, None]) & valid_rows[
            None, :finish
        ]
        weights = jnp.where(allowed[None], weights, 0.0).astype(jnp.bfloat16)
        pieces.append(
            jnp.einsum("hij,jhd->ihd", weights, values[:finish], preferred_element_type=jnp.float32)
        )
    local_sum = jnp.concatenate(pieces, axis=0)
    attended = rms_rows(carried + local_sum, gains)
    attended = (
        jnp.where(valid_rows[:, None, None], attended, 0.0)
        .astype(jnp.bfloat16)
        .reshape(STRETCH, head_count * DH)
    )
    key_phi = jnp.where(
        valid_rows[:, None, None], features(key_feats.astype(jnp.float32)), 0.0
    ).astype(jnp.bfloat16)
    state_next = state_old + jnp.einsum(
        "jhd,jhp->hdp", values, key_phi, preferred_element_type=jnp.float32
    )
    stretch_part = jnp.dot(attended, out_weight, preferred_element_type=jnp.float32).astype(
        jnp.bfloat16
    )
    dec_normed = rms_rows(decode_tokens[0], norm_gain).astype(jnp.bfloat16)
    dec_conved = convolve(decode_tail[0], dec_normed[:, None, :], conv_taps)[:, 0, :]
    dec_qkv = jnp.dot(dec_conved, w_flat, preferred_element_type=jnp.float32).astype(jnp.bfloat16)
    owners = decode_owner[0, :, 0]
    slots_here = decode_slot[0]
    groups = lax.axis_size("tok")
    capacity = max(2, 2 * DEC // groups)
    earlier = jnp.arange(DEC)[None, :] < jnp.arange(DEC)[:, None]
    same_owner = owners[None, :] == owners[:, None]
    rank_in = jnp.sum(earlier & same_owner, axis=1)
    target = owners * capacity + rank_in
    placing = jnp.arange(groups * capacity)[:, None] == target[None, :]
    sent_rows = jnp.dot(
        placing.astype(jnp.bfloat16), dec_qkv, preferred_element_type=jnp.float32
    ).astype(jnp.bfloat16)
    sent_rows = sent_rows.reshape(groups, capacity, head_count * block_width)
    sent_slots = jnp.sum(jnp.where(placing, slots_here[None, :] + 1, 0), axis=1) - 1
    sent_slots = sent_slots.reshape(groups, capacity, 1).astype(jnp.bfloat16)
    sent_rows = jnp.concatenate([sent_rows, sent_slots], axis=2)
    item_rows = lax.all_to_all(sent_rows, "tok", split_axis=0, concat_axis=0, tiled=True)
    item_slots = item_rows[:, :, -1].astype(jnp.int32)
    item_rows = item_rows[:, :, :-1]
    item_count = item_rows.shape[1]
    flat_out = decode_items(
        item_rows.reshape(groups * item_count, head_count * block_width),
        item_slots.reshape(groups * item_count),
        state_cache[0],
        out_gain,
        head_count,
    )
    served = flat_out.reshape(groups, item_count, head_count * DH)
    returned = lax.all_to_all(served, "tok", split_axis=0, concat_axis=0, tiled=True)
    dec_attended = jnp.dot(
        jnp.transpose(placing).astype(jnp.bfloat16),
        returned.reshape(groups * capacity, head_count * DH),
        preferred_element_type=jnp.float32,
    ).astype(jnp.bfloat16)
    dec_part = jnp.dot(dec_attended, out_weight, preferred_element_type=jnp.float32).astype(
        jnp.bfloat16
    )
    heads = lax.axis_size("head")
    pad_rows = 16
    dec_part = dec_part.reshape(heads, DEC // heads, D)
    dec_part = jnp.pad(dec_part, ((0, 0), (0, pad_rows - DEC // heads), (0, 0)))
    both = jnp.concatenate([stretch_part.reshape(heads, rows_own, D), dec_part], axis=1)
    summed = lax.psum_scatter(
        both.reshape(heads * (rows_own + pad_rows), D), "head", scatter_dimension=0, tiled=True
    )
    stretch_out = summed[:rows_own]
    decode_out = summed[rows_own : rows_own + DEC // heads]
    return (stretch_out[None], decode_out[None], state_next[None])


def solution(mesh):
    in_specs = (
        P("tok", "head", None),
        P("tok", None, None),
        P("tok", None, None),
        P("tok", None, None, None),
        P(),
        P(),
        P(None, "head", None),
        P("head"),
        P("head", None),
        P("tok", None, "head", None, None),
        P("tok"),
        P("tok"),
        P("tok", None),
        P("tok", None, None),
    )
    out_specs = (P("tok", "head", None), P("tok", "head", None), P("tok", "head", None, None))
    return jax.shard_map(local, mesh=mesh, in_specs=in_specs, out_specs=out_specs, check_vma=False)
```

profile of v0, /device:TPU:2, one launch (start us, length us, event | category | flops | bytes accessed | tf_op | source)
XLA Modules:
  0.0 199.8 jit_solution(16442440949846528474)
XLA Ops:
  7.3 1.2 fusion.39
  8.5 1.1 fusion.41
  9.6 3.4 %collective-permute-start = (bf16[2,1792]{1,0:T(2,128)(2,1)S(1)}, bf16[2,1792]{1,0:T(2,128)(2,1)S(1)}, u32[]{:S(2)}, u32[]{:S(2)}) collective-permute-start(bf16[2,1792]{1,0:T(2,128)(2,1)S(1)} %slice.116), channel_id=1, source_target_pairs={{0,32},{32,64},{64,96},{96,128},{128,160},{160,192},{192,224},{224... | collective-permute-start | bytes 21512 | tf_op jit(solution)/shard_map/ppermute | solution.py:17
  13.0 0.9 slice_reduce_fusion.2
  14.0 4.4 %collective-permute-done = bf16[2,1792]{1,0:T(2,128)(2,1)S(1)} collective-permute-done((bf16[2,1792]{1,0:T(2,128)(2,1)S(1)}, bf16[2,1792]{1,0:T(2,128)(2,1)S(1)}, u32[]{:S(2)}, u32[]{:S(2)}) %collective-permute-start) | collective-permute-done | bytes 7200 | tf_op jit(solution)/shard_map/ppermute | solution.py:17
  18.4 0.7 broadcast_select_fusion
  19.2 0.8 fusion.43
  20.1 0.2 convert_reduce_fusion.1
  20.9 0.4 convolution_convert_fusion.3
  21.4 0.7 pad_maximum_fusion
  22.1 12.2 %all-to-all-start = ((bf16[32,2,145]{2,1,0:T(2,128)(2,1)}), bf16[32,2,145]{2,1,0:T(2,128)(2,1)S(1)}, u32[]{:S(2)}, u32[]{:S(2)}) async-start(bf16[32,2,145]{2,1,0:T(2,128)(2,1)} %pad_maximum_fusion), calls=%async_computation | async-start | bytes 65536 | tf_op jit(solution)/shard_map/all_to_all | solution.py:160
  35.7 11.6 %all-to-all-done = bf16[32,2,145]{2,1,0:T(2,128)(2,1)S(1)} async-done(((bf16[32,2,145]{2,1,0:T(2,128)(2,1)}), bf16[32,2,145]{2,1,0:T(2,128)(2,1)S(1)}, u32[]{:S(2)}, u32[]{:S(2)}) %all-to-all-start) | async-done | bytes 18592 | tf_op jit(solution)/shard_map/all_to_all | solution.py:160
  47.3 0.7 convert_reduce_fusion
  48.5 0.7 copy.42
  49.3 2.6 %fusion.2 = f32[64,16,112]{2,0,1:T(8,128)S(1)} fusion(f32[1,16,1,112,273]{3,2,4,1,0:T(1,128)S(1)} %copy-done.1, f32[64,1,256]{2,0,1:T(8,128)} %copy.42, f32[64,1,16]{2,0,1:T(8,128)S(1)} %get-tuple-element.20, f32[273]{0:T(512)S(1)} %pad.10.clone), kind=kOutput, calls=%fused_computation.4 | convolution fusion | flops 375752832 | bytes 2486340 | tf_op jit(solution)/shard_map/nhp,shdp->nshd/dot_general | solution.py:51
  51.9 0.7 fusion.27
  52.8 0.7 multiply_convert_fusion
  53.5 3.8 %all-to-all-start.1 = ((bf16[32,2,112]{2,1,0:T(2,128)(2,1)}), bf16[32,2,112]{2,1,0:T(2,128)(2,1)S(1)}, u32[]{:S(2)}, u32[]{:S(2)}) async-start(bf16[32,2,112]{2,1,0:T(2,128)(2,1)} %bitcast.39), calls=%async_computation.1 | async-start | bytes 32768 | tf_op jit(solution)/shard_map/all_to_all | solution.py:172
  57.5 12.3 %all-to-all-done.1 = bf16[32,2,112]{2,1,0:T(2,128)(2,1)S(1)} async-done(((bf16[32,2,112]{2,1,0:T(2,128)(2,1)}), bf16[32,2,112]{2,1,0:T(2,128)(2,1)S(1)}, u32[]{:S(2)}, u32[]{:S(2)}) %all-to-all-start.1) | async-done | bytes 14368 | tf_op jit(solution)/shard_map/all_to_all | solution.py:172
  69.7 0.4 convolution_convert_fusion.1
  70.1 15.6 %all-gather.2.cloned.1.call-done = bf16[1024,1792]{1,0:T(8,128)(2,1)} async-done(((bf16[64,1792]{1,0:T(8,128)(2,1)}), bf16[1024,1792]{1,0:T(8,128)(2,1)}) %all-gather.2.cloned.1.call-update) | async-done | bytes 3670032 | tf_op jit(solution)/shard_map/all_gather | solution.py:89
  85.7 3.4 %fusion.8 = bf16[1024,1,144]{0,2,1:T(8,128)(2,1)S(1)} fusion(bf16[1024,1792]{1,0:T(8,128)(2,1)} %all-gather.2.cloned.1.call-done, bf16[1792,1,144]{0,2,1:T(8,128)(2,1)S(1)} %copy-done), kind=kOutput, calls=%fused_computation.15 | convolution fusion | flops 528629760 | bytes 4481024 | tf_op jit(solution)/shard_map/dot_general | solution.py:88
  89.1 1.1 fusion.9
  90.3 0.7 convolution_bitcast_fusion.1
  91.0 1.2 multiply_reduce_fusion
  92.2 1.2 convolution_convert_fusion
  93.5 2.4 %fusion.1 = bf16[16,80,1792]{2,1,0:T(8,128)(2,1)} fusion(bf16[16,2,1792]{2,1,0:T(2,128)(2,1)S(1)} %reshape.515, bf16[16,64,1792]{2,1,0:T(8,128)(2,1)S(1)} %bitcast.135), kind=kLoop, calls=%fused_computation.2 | loop fusion | flops 13762560 | bytes 8372224 | tf_op jit(solution)/shard_map/concatenate | solution.py:185
  96.0 0.4 fusion.14
  96.5 0.8 copy.45
  97.3 92.7 %reduce-scatter.2.cloned.1.call-done = bf16[80,1792]{1,0:T(8,128)(2,1)} async-done(((bf16[1280,1792]{1,0:T(8,128)(2,1)}), bf16[80,1792]{1,0:T(8,128)(2,1)}) %reduce-scatter.2.cloned.1.call-update) | async-done | bytes 286736 | tf_op jit(solution)/shard_map/reduce_scatter | solution.py:186
  190.0 1.3 slice_bitcast_fusion.16
  191.4 1.6 slice_bitcast_fusion
  (63 shorter events, 1.9 us)
Async XLA Ops:
  7.2 13.7 %copy-start = (bf16[1792,1,144]{0,2,1:T(8,128)(2,1)S(1)}, bf16[1792,1,144]{0,2,1:T(8,128)(2,1)}, u32[]{:S(2)}) copy-start(bf16[1792,1,144]{0,2,1:T(8,128)(2,1)} %param.20) | copy-start | bytes 1548292
  7.2 13.5 %copy-start.5 = (f32[1792]{0:T(1024)S(1)}, f32[1792]{0:T(1024)}, u32[]{:S(2)}) copy-start(f32[1792]{0:T(1024)} %param.18) | copy-start | bytes 21508
  7.2 12.9 %copy-start.9 = (s32[1,32,1]{1,2,0:T(1,128)S(1)}, s32[1,32,1]{1,2,0:T(1,128)}, u32[]{:S(2)}) copy-start(s32[1,32,1]{1,2,0:T(1,128)} %param.27) | copy-start | bytes 388
  7.2 13.0 %copy-start.8 = (s32[1,32]{1,0:T(1,128)S(1)}, s32[1,32]{1,0:T(1,128)}, u32[]{:S(2)}) copy-start(s32[1,32]{1,0:T(1,128)} %param.26) | copy-start | bytes 388
  7.2 13.3 %copy-start.4 = (bf16[1,32,2,1792]{3,2,1,0:T(2,128)(2,1)S(1)}, bf16[1,32,2,1792]{3,2,1,0:T(2,128)(2,1)}, u32[]{:S(2)}) copy-start(bf16[1,32,2,1792]{3,2,1,0:T(2,128)(2,1)} %param.17) | copy-start | bytes 688132
  7.2 13.3 %copy-start.3 = (bf16[1,32,1792]{2,1,0:T(8,128)(2,1)S(1)}, bf16[1,32,1792]{2,1,0:T(8,128)(2,1)}, u32[]{:S(2)}) copy-start(bf16[1,32,1792]{2,1,0:T(8,128)(2,1)} %param.16) | copy-start | bytes 344068
  7.2 78.5 %all-gather.2.cloned.1.call-start = ((), (), s32[]{:S(2)}) async-start(), calls=%async_computation.3 | async-start | bytes 3899392 | tf_op jit(solution)/shard_map/all_gather | solution.py:89
  9.6 8.8 %collective-permute-start = (bf16[2,1792]{1,0:T(2,128)(2,1)S(1)}, bf16[2,1792]{1,0:T(2,128)(2,1)S(1)}, u32[]{:S(2)}, u32[]{:S(2)}) collective-permute-start(bf16[2,1792]{1,0:T(2,128)(2,1)S(1)} %slice.116), channel_id=1, source_target_pairs={{0,32},{32,64},{64,96},{96,128},{128,160},{160,192},{192,224},{224... | collective-permute-start | bytes 21512 | tf_op jit(solution)/shard_map/ppermute | solution.py:17
  19.2 16.5 %copy-start.1 = (f32[1,16,1,112,273]{3,2,4,1,0:T(1,128)S(1)}, f32[1,16,1,112,273]{3,2,4,1,0:T(1,128)}, u32[]{:S(2)}) copy-start(f32[1,16,1,112,273]{3,2,4,1,0:T(1,128)} %param.23) | copy-start | bytes 5870596
  22.1 25.2 %all-to-all-start = ((bf16[32,2,145]{2,1,0:T(2,128)(2,1)}), bf16[32,2,145]{2,1,0:T(2,128)(2,1)S(1)}, u32[]{:S(2)}, u32[]{:S(2)}) async-start(bf16[32,2,145]{2,1,0:T(2,128)(2,1)} %pad_maximum_fusion), calls=%async_computation | async-start | bytes 65536 | tf_op jit(solution)/shard_map/all_to_all | solution.py:160
  35.7 17.1 %copy-start.7 = (f32[112]{0:T(128)S(1)}, f32[112]{0:T(128)}, u32[]{:S(2)}) copy-start(f32[112]{0:T(128)} %param.21) | copy-start | bytes 1348
  48.1 21.6 %copy-start.2 = (bf16[112,1792]{1,0:T(8,128)(2,1)S(1)}, bf16[112,1792]{1,0:T(8,128)(2,1)}, u32[]{:S(2)}) copy-start(bf16[112,1792]{1,0:T(8,128)(2,1)} %param.22) | copy-start | bytes 1204228
  53.5 16.2 %all-to-all-start.1 = ((bf16[32,2,112]{2,1,0:T(2,128)(2,1)}), bf16[32,2,112]{2,1,0:T(2,128)(2,1)S(1)}, u32[]{:S(2)}, u32[]{:S(2)}) async-start(bf16[32,2,112]{2,1,0:T(2,128)(2,1)} %bitcast.39), calls=%async_computation.1 | async-start | bytes 32768 | tf_op jit(solution)/shard_map/all_to_all | solution.py:172
  57.3 132.7 %reduce-scatter.2.cloned.1.call-start = ((), (), s32[]{:S(2)}) async-start(), calls=%async_computation.4 | async-start | bytes 4874240 | tf_op jit(solution)/shard_map/reduce_scatter | solution.py:186
  57.4 31.6 %copy-start.6 = (s32[1024]{0:T(1024)}, s32[1024]{0:T(1024)S(1)}, u32[]{:S(2)}) copy-start(s32[1024]{0:T(1024)S(1)} %iota.31) | copy-start | bytes 12292
  89.1 1.2 slice-start
Sparse Core Ops, SparseCore 0:
  20.2 65.4 all-gather.1
  96.0 93.9 reduce-scatter.1
where the time goes:
time: 200 us
  waiting for transfers between devices  137 us (68%)
  starting transfers between devices  19.6 us (10%)
  between operations  15.8 us (8%)
  matrix products  12.1 us (6%)
  other arithmetic  9.75 us (5%)
  local copies, waits for them, and re-layouts  6 us (3%)
    reduce_scatter x1, waiting for transfers between devices, local(): lax.psum_scatter(both.reshape(heads * (rows_own + pad_rows), D), 'head',...  92.7 us
    all_gather x1, waiting for transfers between devices, local(): lax.all_gather(conved, 'head', axis=0, tiled=True)  15.6 us
    all_to_all x1, waiting for transfers between devices, local(): lax.all_to_all(served, 'tok', split_axis=0, concat_axis=0, tiled=True)  12.3 us
    all_to_all x1, starting transfers between devices, local(): lax.all_to_all(sent_rows, 'tok', split_axis=0, concat_axis=0, tiled=True)  12.2 us
    all_to_all x1, waiting for transfers between devices, local(): lax.all_to_all(sent_rows, 'tok', split_axis=0, concat_axis=0, tiled=True)  11.6 us
    ppermute x1, waiting for transfers between devices, from_behind(): return lax.ppermute(array, axis, pairs)  4.44 us
  transfers between devices with their start and end apart: 5, of which 5 were waited for; matrix products, arithmetic and copies ran while one was open for 5% of the time, Pallas kernels for 0%

commit v1 on v0

--- a/solution.py
+++ b/solution.py
@@ -9,6 +9,11 @@
 F = 16
 STRETCH = 1024
 DEC = 32
+
+
+def gather_by_exchange(x, axis, dim):
+    copies = jnp.concatenate([x] * lax.axis_size(axis), axis=dim)
+    return lax.all_to_all(copies, axis, dim, dim, tiled=True)
 
 
 def from_behind(array, axis, by):
@@ -86,9 +91,7 @@
     rim_rows = jnp.where(first_dev, stretch_tail[0], rim_rows)
     conved = convolve(rim_rows, normed, conv_taps)
     grouped = jnp.dot(
-        lax.all_gather(conved, "head", axis=0, tiled=True),
-        w_flat,
-        preferred_element_type=jnp.float32,
+        gather_by_exchange(conved, "head", 0), w_flat, preferred_element_type=jnp.float32
     ).astype(jnp.bfloat16)
     grouped = grouped.reshape(STRETCH, head_count, block_width)
     queries = grouped[:, :, :F]

time: 200 us -> 243 us (1.22)
  starting transfers between devices: 19.6 us -> 36.3 us
  local copies, waits for them, and re-layouts: 6 us -> 17.7 us
  waiting for transfers between devices: 137 us -> 148 us
  other arithmetic: 9.75 us -> 12.8 us
    all_to_all x0 -> x1, waiting for transfers between devices: none -> 48.8 us  [gather_by_exchange(): return lax.all_to_all(copies, axis, dim, dim, tiled=True)]
    all_gather x1 -> x0, waiting for transfers between devices: 15.6 us -> none  [local(): lax.all_gather(conved, 'head', axis=0, tiled=True)]
    unnamed x22 -> x30, local copies, waits for them, and re-layouts: 0.89 us -> 12.5 us
    all_to_all x1, waiting for transfers between devices: 11.6 us -> 2.09 us  [local(): lax.all_to_all(sent_rows, 'tok', split_axis=0, concat_axis=0, tiled=True)]
    reduce_scatter x1, waiting for transfers between devices: 92.7 us -> 85.3 us  [local(): lax.psum_scatter(both.reshape(heads * (rows_own + pad_rows), D), 'head',...]
    all_to_all x0 -> x1, starting transfers between devices: none -> 7.31 us  [gather_by_exchange(): return lax.all_to_all(copies, axis, dim, dim, tiled=True)]
    all_to_all x1, starting transfers between devices: 3.83 us -> 10.1 us  [local(): lax.all_to_all(served, 'tok', split_axis=0, concat_axis=0, tiled=True)]
    ppermute x1, waiting for transfers between devices: 4.44 us -> 0.01 us  [from_behind(): return lax.ppermute(array, axis, pairs)]
  transfers between devices with their start and end apart: 5 -> 5, of which waited for: 5 -> 4; matrix products, arithmetic and copies ran while one was open for 5% -> 9% of each run, Pallas kernels for 0% -> 0%
where the time goes in v1:
time: 243 us; the launch traced here: 242 us
  waiting for transfers between devices  148 us (61%)
  starting transfers between devices  36.3 us (15%)
  local copies, waits for them, and re-layouts  17.7 us (7%)
  between operations  15.8 us (7%)
  other arithmetic  12.8 us (5%)
  matrix products  11.3 us (5%)
    reduce_scatter x1, waiting for transfers between devices, local(): lax.psum_scatter(both.reshape(heads * (rows_own + pad_rows), D), 'head',...  85.3 us
    all_to_all x1, waiting for transfers between devices, gather_by_exchange(): return lax.all_to_all(copies, axis, dim, dim, tiled=True)  48.8 us
    all_to_all x1, starting transfers between devices, local(): lax.all_to_all(sent_rows, 'tok', split_axis=0, concat_axis=0, tiled=True)  15.5 us
    unnamed x30, local copies, waits for them, and re-layouts  12.5 us
    all_to_all x1, waiting for transfers between devices, local(): lax.all_to_all(served, 'tok', split_axis=0, concat_axis=0, tiled=True)  11.7 us
    all_to_all x1, starting transfers between devices, local(): lax.all_to_all(served, 'tok', split_axis=0, concat_axis=0, tiled=True)  10.1 us
    all_to_all x1, starting transfers between devices, gather_by_exchange(): return lax.all_to_all(copies, axis, dim, dim, tiled=True)  7.31 us
  transfers between devices with their start and end apart: 5, of which 4 were waited for; matrix products, arithmetic and copies ran while one was open for 9% of the time, Pallas kernels for 0%

profile of v1, /device:TPU:2, one launch (start us, length us, event | category | flops | bytes accessed | tf_op | source)
XLA Modules:
  0.0 241.9 jit_solution(7615202542930090720)
XLA Ops:
  7.2 1.1 fusion.39
  8.3 1.1 fusion.41
  9.4 3.4 %collective-permute-start = (bf16[2,1792]{1,0:T(2,128)(2,1)S(1)}, bf16[2,1792]{1,0:T(2,128)(2,1)S(1)}, u32[]{:S(2)}, u32[]{:S(2)}) collective-permute-start(bf16[2,1792]{1,0:T(2,128)(2,1)S(1)} %slice.116), channel_id=1, source_target_pairs={{0,32},{32,64},{64,96},{96,128},{128,160},{160,192},{192,224},{224... | collective-permute-start | bytes 21512 | tf_op jit(solution)/shard_map/ppermute | solution.py:22
  13.5 0.9 convert_reduce_fusion.1
  15.2 1.0 fusion.48
  16.4 0.9 slice_reduce_fusion.2
  17.3 1.0 fusion.47
  18.3 1.0 copy.67
  20.5 15.5 %all-to-all-start.1 = ((bf16[32,2,145]{2,1,0:T(2,128)(2,1)}), bf16[32,2,145]{2,1,0:T(2,128)(2,1)S(1)}, u32[]{:S(2)}, u32[]{:S(2)}) async-start(bf16[32,2,145]{2,1,0:T(2,128)(2,1)} %pad_maximum_fusion), calls=%async_computation.1 | async-start | bytes 65536 | tf_op jit(solution)/shard_map/all_to_all | solution.py:163
  36.2 0.8 constant_dynamic-update-slice_fusion.15
  37.0 0.7 constant_dynamic-update-slice_fusion.14
  39.1 0.7 constant_dynamic-update-slice_fusion.11
  39.8 0.7 constant_dynamic-update-slice_fusion.10
  42.0 0.7 constant_dynamic-update-slice_fusion.7
  46.2 0.7 constant_dynamic-update-slice_fusion.1
  46.9 2.1 all-to-all-done.1
  50.4 1.8 fusion.2
  53.8 10.1 %all-to-all-start.2 = ((bf16[32,2,112]{2,1,0:T(2,128)(2,1)}), bf16[32,2,112]{2,1,0:T(2,128)(2,1)S(1)}, u32[]{:S(2)}, u32[]{:S(2)}) async-start(bf16[32,2,112]{2,1,0:T(2,128)(2,1)} %bitcast.41), calls=%async_computation.2 | async-start | bytes 32768 | tf_op jit(solution)/shard_map/all_to_all | solution.py:175
  63.9 0.7 constant_dynamic-update-slice_fusion
  64.6 11.7 %all-to-all-done.2 = bf16[32,2,112]{2,1,0:T(2,128)(2,1)S(1)} async-done(((bf16[32,2,112]{2,1,0:T(2,128)(2,1)}), bf16[32,2,112]{2,1,0:T(2,128)(2,1)S(1)}, u32[]{:S(2)}, u32[]{:S(2)}) %all-to-all-start.2) | async-done | bytes 14368 | tf_op jit(solution)/shard_map/all_to_all | solution.py:175
  76.3 7.3 %all-to-all-start = ((bf16[16,64,1792]{2,1,0:T(8,128)(2,1)}), bf16[16,64,1792]{2,1,0:T(8,128)(2,1)}, u32[]{:S(2)}, u32[]{:S(2)}) async-start(bf16[16,64,1792]{2,1,0:T(8,128)(2,1)} %bitcast.5), calls=%async_computation | async-start | bytes 7340032 | tf_op jit(solution)/shard_map/all_to_all | solution.py:16
  85.5 48.8 %all-to-all-done = bf16[16,64,1792]{2,1,0:T(8,128)(2,1)} async-done(((bf16[16,64,1792]{2,1,0:T(8,128)(2,1)}), bf16[16,64,1792]{2,1,0:T(8,128)(2,1)}, u32[]{:S(2)}, u32[]{:S(2)}) %all-to-all-start) | async-done | bytes 3670048 | tf_op jit(solution)/shard_map/all_to_all | solution.py:16
  134.3 3.4 %fusion.8 = bf16[1024,1,144]{0,2,1:T(8,128)(2,1)S(1)} fusion(bf16[1024,1792]{1,0:T(8,128)(2,1)} %bitcast.6, bf16[1792,1,144]{0,2,1:T(8,128)(2,1)S(1)} %copy-done), kind=kOutput, calls=%fused_computation.15 | convolution fusion | flops 528629760 | bytes 4481024 | tf_op jit(solution)/shard_map/dot_general | solution.py:93
  137.7 1.1 fusion.9
  139.7 1.2 multiply_reduce_fusion
  140.9 1.2 convolution_convert_fusion
  142.1 2.4 fusion.1
  144.7 0.8 copy-done.4
  145.9 0.8 copy.45
  146.7 85.3 %reduce-scatter.2.cloned.1.call-done = bf16[80,1792]{1,0:T(8,128)(2,1)} async-done(((bf16[1280,1792]{1,0:T(8,128)(2,1)}), bf16[80,1792]{1,0:T(8,128)(2,1)}) %reduce-scatter.2.cloned.1.call-update) | async-done | bytes 286736 | tf_op jit(solution)/shard_map/reduce_scatter | solution.py:189
  232.0 1.3 slice_bitcast_fusion.16
  233.4 1.6 slice_bitcast_fusion
  (70 shorter events, 14.0 us)
Async XLA Ops:
  7.2 12.2 %copy-start = (bf16[1792,1,144]{0,2,1:T(8,128)(2,1)S(1)}, bf16[1792,1,144]{0,2,1:T(8,128)(2,1)}, u32[]{:S(2)}) copy-start(bf16[1792,1,144]{0,2,1:T(8,128)(2,1)} %param.20) | copy-start | bytes 1548292
  7.2 28.9 %copy-start.5 = (bf16[1,2,1792]{2,1,0:T(2,128)(2,1)S(1)}, bf16[1,2,1792]{2,1,0:T(2,128)(2,1)}, u32[]{:S(2)}) copy-start(bf16[1,2,1792]{2,1,0:T(2,128)(2,1)} %param.15) | copy-start | bytes 21508
  9.4 26.6 %collective-permute-start = (bf16[2,1792]{1,0:T(2,128)(2,1)S(1)}, bf16[2,1792]{1,0:T(2,128)(2,1)S(1)}, u32[]{:S(2)}, u32[]{:S(2)}) collective-permute-start(bf16[2,1792]{1,0:T(2,128)(2,1)S(1)} %slice.116), channel_id=1, source_target_pairs={{0,32},{32,64},{64,96},{96,128},{128,160},{160,192},{192,224},{224... | collective-permute-start | bytes 21512 | tf_op jit(solution)/shard_map/ppermute | solution.py:22
  20.5 28.5 %all-to-all-start.1 = ((bf16[32,2,145]{2,1,0:T(2,128)(2,1)}), bf16[32,2,145]{2,1,0:T(2,128)(2,1)S(1)}, u32[]{:S(2)}, u32[]{:S(2)}) async-start(bf16[32,2,145]{2,1,0:T(2,128)(2,1)} %pad_maximum_fusion), calls=%async_computation.1 | async-start | bytes 65536 | tf_op jit(solution)/shard_map/all_to_all | solution.py:163
  37.0 13.3 %copy-start.1 = (f32[1,16,1,112,273]{3,2,4,1,0:T(1,128)S(1)}, f32[1,16,1,112,273]{3,2,4,1,0:T(1,128)}, u32[]{:S(2)}) copy-start(f32[1,16,1,112,273]{3,2,4,1,0:T(1,128)} %param.23) | copy-start | bytes 5870596
  42.7 10.4 %copy-start.6 = (f32[112]{0:T(128)S(1)}, f32[112]{0:T(128)}, u32[]{:S(2)}) copy-start(f32[112]{0:T(128)} %param.21) | copy-start | bytes 1348
  53.8 22.5 %all-to-all-start.2 = ((bf16[32,2,112]{2,1,0:T(2,128)(2,1)}), bf16[32,2,112]{2,1,0:T(2,128)(2,1)S(1)}, u32[]{:S(2)}, u32[]{:S(2)}) async-start(bf16[32,2,112]{2,1,0:T(2,128)(2,1)} %bitcast.41), calls=%async_computation.2 | async-start | bytes 32768 | tf_op jit(solution)/shard_map/all_to_all | solution.py:175
  76.3 8.8 %copy-start.2 = (bf16[112,1792]{1,0:T(8,128)(2,1)S(1)}, bf16[112,1792]{1,0:T(8,128)(2,1)}, u32[]{:S(2)}) copy-start(bf16[112,1792]{1,0:T(8,128)(2,1)} %param.22) | copy-start | bytes 1204228
  76.3 58.0 %all-to-all-start = ((bf16[16,64,1792]{2,1,0:T(8,128)(2,1)}), bf16[16,64,1792]{2,1,0:T(8,128)(2,1)}, u32[]{:S(2)}, u32[]{:S(2)}) async-start(bf16[16,64,1792]{2,1,0:T(8,128)(2,1)} %bitcast.5), calls=%async_computation | async-start | bytes 7340032 | tf_op jit(solution)/shard_map/all_to_all | solution.py:16
  83.6 148.5 %reduce-scatter.2.cloned.1.call-start = ((), (), s32[]{:S(2)}) async-start(), calls=%async_computation.4 | async-start | bytes 4874240 | tf_op jit(solution)/shard_map/reduce_scatter | solution.py:189
  137.7 2.0 copy-start.3
  144.5 1.0 copy-start.4
Sparse Core Ops, SparseCore 0:
  144.7 87.3 reduce-scatter.1
